TPU v7x, 256 devices: a whole 4x4x8 slice. The times are simulated.
256 devices in a mesh: panel: 16 (over y_hi, z), dir: 8 (over x, core), freq: 2 (over y_lo).
Axes of the slice: x: 4, y: 4 (y_hi: 2, y_lo: 2; y = y_hi * 2 + y_lo), z: 8, core: 2. Of those that a mesh axis runs over, the one named last changes fastest.
Arguments:
- sources: bfloat16 [4, 2, 64, 65536], P('freq', None, None, 'panel'), may hold values from -0.046875 to 0.046875
- panel_geom: float32 [4, 65536], P(None, 'panel'), may hold values from -150 to 150, as said below
- drift_cot: float32 [4, 64], P('freq'), may hold values from -4 to 4
- freq_index: int32 [4], P('freq'), may hold values from 0 to 511
- heading_dir: int32 [64], replicated, may hold values from 0 to 4095
Outputs:
- source_grad: float32 [4, 2, 64, 65536], P('freq', None, None, ('panel', 'dir'))
- geom_grad: float32 [4, 65536], P(None, ('panel', 'dir'))
Inputs may be any that keep to these rules, and one draw needn't show every extreme that they name: `panel_geom`: rows are panel centre x, y, z in metres, z at or below the water line, and panel area from 0.5 to 2.
All inputs are finite; a program needn't handle non-finite values.
Results may differ from a plain program's by a relative error of at most 0.00042.
Values may be sent and summed in bfloat16 or wider, within the bound.
A program may use at most 64 MiB of HBM per device.

v0:
```python
import math
import jax
import jax.numpy as jnp
from jax import lax
from jax.sharding import PartitionSpec as P

ND = 4096
FREQS = 512
gravity = 9.81
omega_low = 0.6
omega_span = 0.8
drift_gain = 5.0
cross_gain = 0.5
shape_scale = 100.0


def wave_numbers(freq_index):
    omega = omega_low + omega_span * freq_index.astype(jnp.float32) / FREQS
    return omega * omega / gravity


def direction_angles(dir_ids):
    return dir_ids.astype(jnp.float32) * (2.0 * math.pi / ND)


def phase_terms(geometry, wave, angles):
    amplitude = geometry[3] * jnp.exp(wave * geometry[2])
    phase = wave * (
        geometry[0][:, None] * jnp.cos(angles)[None, :]
        + geometry[1][:, None] * jnp.sin(angles)[None, :]
    )
    return (amplitude[:, None] * jnp.cos(phase), -amplitude[:, None] * jnp.sin(phase))


def kochin_block(sig, geometry, wave, dir_ids):
    heads = sig.shape[1]
    real, imag = phase_terms(geometry, wave, direction_angles(dir_ids))
    width = real.shape[1]
    phases = jnp.concatenate([real, imag], 1).astype(jnp.bfloat16)
    prod = jnp.dot(sig.reshape(2 * heads, sig.shape[2]), phases, preferred_element_type=jnp.float32)
    kreal = prod[:heads, :width] - prod[heads:, width:]
    kimag = prod[:heads, width:] + prod[heads:, :width]
    return jnp.stack([kreal, kimag])


def cotangent(kochin, wave, dir_ids, weight, heading_dir):
    angles = direction_angles(dir_ids)
    slope = -drift_gain * wave / math.sqrt(ND)
    beta = direction_angles(heading_dir)
    hit = (dir_ids[None, :] == heading_dir[:, None]).astype(jnp.float32)
    along = 2.0 * slope * jnp.cos(angles)[None, :]
    real_part = weight[:, None] * (along * kochin[0] - cross_gain * jnp.cos(beta)[:, None] * hit)
    imag_part = weight[:, None] * (along * kochin[1])
    return jnp.stack([real_part, imag_part]).astype(jnp.bfloat16)


def backward_block(sig, geometry, wave, dir_ids, cot):
    heads = sig.shape[1]
    angles = direction_angles(dir_ids)
    real, imag = phase_terms(geometry, wave, angles)
    width = real.shape[1]
    phases = jnp.concatenate([real, imag], 1).astype(jnp.bfloat16)
    mixed = jnp.concatenate(
        [jnp.concatenate([cot[0], cot[1]], 1), jnp.concatenate([cot[1], -cot[0]], 1)], 0
    )
    flat = sig.reshape(2 * heads, sig.shape[2])
    dsig = jnp.dot(mixed, phases.T, preferred_element_type=jnp.float32)
    dphase = jnp.dot(flat.T, mixed, preferred_element_type=jnp.float32)
    d_real = dphase[:, :width]
    d_imag = dphase[:, width:]
    twist = d_real * imag - d_imag * real
    swell = d_real * real + d_imag * imag
    shape = jnp.stack(
        [
            wave * jnp.sum(twist * jnp.cos(angles)[None, :], 1),
            wave * jnp.sum(twist * jnp.sin(angles)[None, :], 1),
            wave * jnp.sum(swell, 1),
            jnp.sum(swell, 1) / geometry[3],
        ]
    )
    return (dsig, shape)


def body(sources, panel_geom, drift_cot, freq_index, heading_dir):
    local_freqs = sources.shape[0]
    heads = sources.shape[2]
    panels = sources.shape[3]
    dir_count = ND // lax.axis_size("dir")
    dir_ids = lax.axis_index("dir") * dir_count + jnp.arange(dir_count, dtype=jnp.int32)
    waves = wave_numbers(freq_index)
    block = min(panels, 512)
    steps = panels // block
    kochin_parts = []
    for freq in range(local_freqs):

        def add_block(step, total):
            start = step * block
            sig = lax.dynamic_slice_in_dim(sources[freq], start, block, 2)
            geometry = lax.dynamic_slice_in_dim(panel_geom, start, block, 1)
            return total + kochin_block(sig, geometry, waves[freq], dir_ids)

        kochin_parts.append(
            lax.fori_loop(0, steps, add_block, jnp.zeros((2, heads, dir_count), jnp.float32))
        )
    partial_kochin = jnp.stack(kochin_parts)
    kochin = lax.psum(partial_kochin, "panel")
    cot = jnp.stack(
        [
            cotangent(kochin[freq], waves[freq], dir_ids, drift_cot[freq], heading_dir)
            for freq in range(local_freqs)
        ]
    )
    grads = []
    shape_total = jnp.zeros((4, panels), jnp.float32)
    for freq in range(local_freqs):

        def back_block(step, carry):
            grads_acc, shape_acc = carry
            start = step * block
            sig = lax.dynamic_slice_in_dim(sources[freq], start, block, 2)
            geometry = lax.dynamic_slice_in_dim(panel_geom, start, block, 1)
            dsig, shape = backward_block(sig, geometry, waves[freq], dir_ids, cot[freq])
            grads_acc = lax.dynamic_update_slice_in_dim(grads_acc, dsig, start, 1)
            old_shape = lax.dynamic_slice_in_dim(shape_acc, start, block, 1)
            shape_acc = lax.dynamic_update_slice_in_dim(shape_acc, old_shape + shape, start, 1)
            return (grads_acc, shape_acc)

        grads_freq, shape_total = lax.fori_loop(
            0, steps, back_block, (jnp.zeros((2 * heads, panels), jnp.float32), shape_total)
        )
        grads.append(grads_freq)
    grads_all = jnp.stack(grads).reshape(local_freqs, 2, heads, panels)
    source_part, shape_part = (
        lax.psum_scatter(grads_all, "dir", scatter_dimension=3, tiled=True),
        lax.psum_scatter(shape_total, "dir", scatter_dimension=1, tiled=True),
    )
    shape_all = lax.psum(shape_part, "freq")
    return (source_part, shape_scale * shape_all)


def solution(mesh):
    return jax.shard_map(
        body,
        mesh=mesh,
        in_specs=(
            P("freq", None, None, "panel"),
            P(None, "panel"),
            P("freq", None),
            P("freq"),
            P(),
        ),
        out_specs=(P("freq", None, None, ("panel", "dir")), P(None, ("panel", "dir"))),
        check_vma=False,
    )
```

profile of v0, /device:TPU:8, one launch (start us, length us, event | category | flops | bytes accessed | tf_op | source)
XLA Modules:
  0.0 536.5 jit_solution(602441275165219904)
XLA Ops:
  7.9 70.9 %while.75 = (s32[]{:T(128)}, f32[2,64,512]{2,1,0:T(8,128)S(1)}, bf16[2,2,64,4096]{3,2,1,0:T(8,128)(2,1)}, f32[4,4096]{1,0:T(4,128)}, f32[2]{0:T(128)S(1)}, /*ind...) while((s32[]{:T(128)}, f32[2,64,512]{2,1,0:T(8,128)S(1)}, ...), condition=%wide.region_3.0_spmd.clone, body=%wide.region_2.0_spmd.clone.sunk | while | flops 138677248 | bytes 6719753 | solution.py:103
  8.6 1.5 constant_dynamic-slice_fusion.23
  10.1 4.9 multiply_convert_fusion.7
  17.4 1.5 constant_dynamic-slice_fusion.23
  18.9 4.9 multiply_convert_fusion.7
  27.8 4.9 multiply_convert_fusion.7
  35.2 1.5 constant_dynamic-slice_fusion.23
  36.7 4.9 multiply_convert_fusion.7
  44.0 1.5 constant_dynamic-slice_fusion.23
  45.5 4.9 multiply_convert_fusion.7
  54.4 4.9 multiply_convert_fusion.7
  63.3 4.9 multiply_convert_fusion.7
  72.1 4.9 multiply_convert_fusion.7
  78.9 58.0 %while.74 = (s32[]{:T(128)}, f32[2,64,512]{2,1,0:T(8,128)S(1)}, bf16[2,2,64,4096]{3,2,1,0:T(8,128)(2,1)}, f32[4,4096]{1,0:T(4,128)}, f32[2]{0:T(128)S(1)}, /*ind...) while((s32[]{:T(128)}, f32[2,64,512]{2,1,0:T(8,128)S(1)}, ...), condition=%wide.region_1.0_spmd.clone, body=%wide.region_0.0_spmd.clone.sunk | while | flops 138677248 | bytes 6719745 | solution.py:103
  79.9 4.4 multiply_convert_fusion.6
  87.2 4.4 multiply_convert_fusion.6
  94.4 4.4 multiply_convert_fusion.6
  101.7 4.4 multiply_convert_fusion.6
  108.9 4.4 multiply_convert_fusion.6
  116.2 4.4 multiply_convert_fusion.6
  123.4 4.4 multiply_convert_fusion.6
  130.7 4.4 multiply_convert_fusion.6
  139.7 157.6 %all-reduce.2.cloned.1.call-done = f32[2,2,64,512]{3,2,1,0:T(8,128)} async-done(((f32[2,2,64,512]{3,2,1,0:T(8,128)}), f32[2,2,64,512]{3,2,1,0:T(8,128)}) %all-reduce.2.cloned.1.call-update) | async-done | bytes 524304 | tf_op jit(solution)/shard_map/psum | solution.py:106
  299.5 1.6 broadcast.578.clone2
  301.1 59.4 %while.72 = (s32[]{:T(128)}, f32[128,4096]{1,0:T(8,128)}, f32[4,4096]{1,0:T(4,128)S(1)}, f32[4,4096]{1,0:T(4,128)S(1)}, f32[2]{0:T(128)S(1)}, /*index=5*/bf16[12...) while((s32[]{:T(128)}, f32[128,4096]{1,0:T(8,128)}, ...), condition=%wide.region_9.10_spmd.clone, body=%wide.region_5.9_spmd.clone.sunk | while | flops 275526656 | bytes 10699039 | solution.py:128
  301.9 5.1 multiply_reduce_fusion.6
  309.4 5.1 multiply_reduce_fusion.6
  316.8 5.1 multiply_reduce_fusion.6
  324.2 5.1 multiply_reduce_fusion.6
  331.6 5.1 multiply_reduce_fusion.6
  339.0 5.1 multiply_reduce_fusion.6
  346.4 5.1 multiply_reduce_fusion.6
  353.9 5.1 multiply_reduce_fusion.6
  360.5 1.6 broadcast.578.clone
  362.1 88.5 %while.73 = (s32[]{:T(128)}, f32[128,4096]{1,0:T(8,128)}, f32[4,4096]{1,0:T(4,128)S(1)}, f32[4,4096]{1,0:T(4,128)S(1)}, f32[2]{0:T(128)S(1)}, /*index=5*/bf16[12...) while((s32[]{:T(128)}, f32[128,4096]{1,0:T(8,128)}, ...), condition=%wide.region_14.15_spmd.clone, body=%wide.region_10.14_spmd.clone.sunk | while | flops 275526656 | bytes 10699047 | solution.py:128
  364.1 5.7 %multiply_reduce_fusion.7 = (f32[512]{0:T(512)S(1)}, f32[512]{0:T(512)S(1)}, f32[512]{0:T(512)S(1)}, bf16[512,512]{1,0:T(8,128)(2,1)S(1)}, bf16[512,512]{1,0:T(8,128)(2,1)S(1)}) fusion(f32[512]{0:T(512)S(1)} %bitcast.240, f32[512]{0:T(512)S(1)} %bitcast.246, f32[512]{0:T(512)S(1)} %neg.91, f32[512,1024]{1,0:T(8,128)S(1)} %fusion.121, ...), kind=kLoop, calls=%fused_computation.39.clone.1 | loop fusion | flops 4979200 | bytes 3164164 | tf_op jit(solution)/shard_map/while/body/eval_jaxpr/reduce_sum | solution.py:75
  375.1 5.7 %multiply_reduce_fusion.7 = (f32[512]{0:T(512)S(1)}, f32[512]{0:T(512)S(1)}, f32[512]{0:T(512)S(1)}, bf16[512,512]{1,0:T(8,128)(2,1)S(1)}, bf16[512,512]{1,0:T(8,128)(2,1)S(1)}) fusion(f32[512]{0:T(512)S(1)} %bitcast.240, f32[512]{0:T(512)S(1)} %bitcast.246, f32[512]{0:T(512)S(1)} %neg.91, f32[512,1024]{1,0:T(8,128)S(1)} %fusion.121, ...), kind=kLoop, calls=%fused_computation.39.clone.1 | loop fusion | flops 4979200 | bytes 3164164 | tf_op jit(solution)/shard_map/while/body/eval_jaxpr/reduce_sum | solution.py:75
  386.2 5.7 %multiply_reduce_fusion.7 = (f32[512]{0:T(512)S(1)}, f32[512]{0:T(512)S(1)}, f32[512]{0:T(512)S(1)}, bf16[512,512]{1,0:T(8,128)(2,1)S(1)}, bf16[512,512]{1,0:T(8,128)(2,1)S(1)}) fusion(f32[512]{0:T(512)S(1)} %bitcast.240, f32[512]{0:T(512)S(1)} %bitcast.246, f32[512]{0:T(512)S(1)} %neg.91, f32[512,1024]{1,0:T(8,128)S(1)} %fusion.121, ...), kind=kLoop, calls=%fused_computation.39.clone.1 | loop fusion | flops 4979200 | bytes 3164164 | tf_op jit(solution)/shard_map/while/body/eval_jaxpr/reduce_sum | solution.py:75
  397.2 5.7 %multiply_reduce_fusion.7 = (f32[512]{0:T(512)S(1)}, f32[512]{0:T(512)S(1)}, f32[512]{0:T(512)S(1)}, bf16[512,512]{1,0:T(8,128)(2,1)S(1)}, bf16[512,512]{1,0:T(8,128)(2,1)S(1)}) fusion(f32[512]{0:T(512)S(1)} %bitcast.240, f32[512]{0:T(512)S(1)} %bitcast.246, f32[512]{0:T(512)S(1)} %neg.91, f32[512,1024]{1,0:T(8,128)S(1)} %fusion.121, ...), kind=kLoop, calls=%fused_computation.39.clone.1 | loop fusion | flops 4979200 | bytes 3164164 | tf_op jit(solution)/shard_map/while/body/eval_jaxpr/reduce_sum | solution.py:75
  408.3 5.7 %multiply_reduce_fusion.7 = (f32[512]{0:T(512)S(1)}, f32[512]{0:T(512)S(1)}, f32[512]{0:T(512)S(1)}, bf16[512,512]{1,0:T(8,128)(2,1)S(1)}, bf16[512,512]{1,0:T(8,128)(2,1)S(1)}) fusion(f32[512]{0:T(512)S(1)} %bitcast.240, f32[512]{0:T(512)S(1)} %bitcast.246, f32[512]{0:T(512)S(1)} %neg.91, f32[512,1024]{1,0:T(8,128)S(1)} %fusion.121, ...), kind=kLoop, calls=%fused_computation.39.clone.1 | loop fusion | flops 4979200 | bytes 3164164 | tf_op jit(solution)/shard_map/while/body/eval_jaxpr/reduce_sum | solution.py:75
  419.4 5.7 %multiply_reduce_fusion.7 = (f32[512]{0:T(512)S(1)}, f32[512]{0:T(512)S(1)}, f32[512]{0:T(512)S(1)}, bf16[512,512]{1,0:T(8,128)(2,1)S(1)}, bf16[512,512]{1,0:T(8,128)(2,1)S(1)}) fusion(f32[512]{0:T(512)S(1)} %bitcast.240, f32[512]{0:T(512)S(1)} %bitcast.246, f32[512]{0:T(512)S(1)} %neg.91, f32[512,1024]{1,0:T(8,128)S(1)} %fusion.121, ...), kind=kLoop, calls=%fused_computation.39.clone.1 | loop fusion | flops 4979200 | bytes 3164164 | tf_op jit(solution)/shard_map/while/body/eval_jaxpr/reduce_sum | solution.py:75
  430.4 5.7 %multiply_reduce_fusion.7 = (f32[512]{0:T(512)S(1)}, f32[512]{0:T(512)S(1)}, f32[512]{0:T(512)S(1)}, bf16[512,512]{1,0:T(8,128)(2,1)S(1)}, bf16[512,512]{1,0:T(8,128)(2,1)S(1)}) fusion(f32[512]{0:T(512)S(1)} %bitcast.240, f32[512]{0:T(512)S(1)} %bitcast.246, f32[512]{0:T(512)S(1)} %neg.91, f32[512,1024]{1,0:T(8,128)S(1)} %fusion.121, ...), kind=kLoop, calls=%fused_computation.39.clone.1 | loop fusion | flops 4979200 | bytes 3164164 | tf_op jit(solution)/shard_map/while/body/eval_jaxpr/reduce_sum | solution.py:75
  441.5 5.7 %multiply_reduce_fusion.7 = (f32[512]{0:T(512)S(1)}, f32[512]{0:T(512)S(1)}, f32[512]{0:T(512)S(1)}, bf16[512,512]{1,0:T(8,128)(2,1)S(1)}, bf16[512,512]{1,0:T(8,128)(2,1)S(1)}) fusion(f32[512]{0:T(512)S(1)} %bitcast.240, f32[512]{0:T(512)S(1)} %bitcast.246, f32[512]{0:T(512)S(1)} %neg.91, f32[512,1024]{1,0:T(8,128)S(1)} %fusion.121, ...), kind=kLoop, calls=%fused_computation.39.clone.1 | loop fusion | flops 4979200 | bytes 3164164 | tf_op jit(solution)/shard_map/while/body/eval_jaxpr/reduce_sum | solution.py:75
  450.5 2.0 copy.11
  452.6 3.9 pad_maximum_fusion
  456.5 30.8 %reduce-scatter.7.cloned.1.call-done = f32[512,4]{1,0:T(8,128)} async-done(((f32[4096,4]{1,0:T(8,128)}), f32[512,4]{1,0:T(8,128)}) %reduce-scatter.7.cloned.1.call-update) | async-done | bytes 8208
  488.4 5.0 psum.15
  494.0 35.9 %reduce-scatter.5.cloned.1.call-done = f32[2,2,64,512]{3,2,1,0:T(8,128)} async-done(((f32[2,2,64,4096]{3,2,1,0:T(8,128)}), f32[2,2,64,512]{3,2,1,0:T(8,128)}) %reduce-scatter.5.cloned.1.call-update) | async-done | bytes 524304 | tf_op jit(solution)/shard_map/reduce_scatter | solution.py:134
  (380 shorter events, 114.8 us)
Async XLA Ops:
  7.2 290.2 %all-reduce.2.cloned.1.call-start = ((), (), s32[]{:S(2)}) async-start(), calls=%async_computation.2 | async-start | bytes 1048576 | tf_op jit(solution)/shard_map/psum | solution.py:106
  78.8 60.8 %copy-start.4 = (s32[64]{0:T(128)S(1)}, s32[64]{0:T(128)}, u32[]{:S(2)}) copy-start(s32[64]{0:T(128)} %param.17) | copy-start | bytes 772
  78.8 60.8 %copy-start.3 = (f32[2,64]{1,0:T(2,128)S(1)}, f32[2,64]{1,0:T(2,128)}, u32[]{:S(2)}) copy-start(f32[2,64]{1,0:T(2,128)} %param.15) | copy-start | bytes 1540
  137.7 163.5 %copy-start = (bf16[2,2,64,4096]{3,2,1,0:T(8,128)(2,1)S(1)}, bf16[2,2,64,4096]{3,2,1,0:T(8,128)(2,1)}, u32[]{:S(2)}) copy-start(bf16[2,2,64,4096]{3,2,1,0:T(8,128)(2,1)} %get-tuple-element.1416) | copy-start | bytes 6291460
  137.7 163.5 %copy-start.2 = (f32[4,4096]{1,0:T(4,128)S(1)}, f32[4,4096]{1,0:T(4,128)}, u32[]{:S(2)}) copy-start(f32[4,4096]{1,0:T(4,128)} %get-tuple-element.1429) | copy-start | bytes 196612
  137.7 349.6 %reduce-scatter.7.cloned.1.call-start = ((), (), s32[]{:S(2)}) async-start(), calls=%async_computation.4 | async-start | bytes 2359296
  450.5 2.1 copy-start.1
  452.5 77.4 %reduce-scatter.5.cloned.1.call-start = ((), (), s32[]{:S(2)}) async-start(), calls=%async_computation.3 | async-start | bytes 4718592 | tf_op jit(solution)/shard_map/reduce_scatter | solution.py:134
Sparse Core Ops, SparseCore 0:
  137.8 159.4 all-reduce.1
  452.7 34.6 reduce-scatter.6
  490.5 39.4 reduce-scatter.4
where the time goes:
time: 539 us; the launch traced here: 536 us
  waiting for transfers between devices  224 us (42%)
  other arithmetic  218 us (40%)
  local copies, waits for them, and re-layouts  52.7 us (10%)
  matrix products  19 us (4%)
  between operations  15.1 us (3%)
    psum x1, waiting for transfers between devices, body(): kochin = lax.psum(partial_kochin, 'panel')  158 us
    reduce_sum x16, other arithmetic, backward_block(): jnp.sum(twist * jnp.cos(angles)[None, :], 1)  85.8 us
    another operation x16, other arithmetic  74.2 us
    reduce_scatter x1, waiting for transfers between devices, body(): lax.psum_scatter(grads_all, 'dir', scatter_dimension=3, tiled=True)  35.9 us
    unnamed x4, waiting for transfers between devices  30.9 us
    slice x32, other arithmetic, phase_terms(): geometry[0][:, None] * jnp.cos(angles)[None, :]  26.9 us
    slice x16, local copies, waits for them, and re-layouts, add_block(): sig = lax.dynamic_slice_in_dim(sources[freq], start, block, 2)  20.7 us
    dynamic_update_slice x32, local copies, waits for them, and re-layouts, back_block(): grads_acc = lax.dynamic_update_slice_in_dim(grads_acc, dsig, start, 1)  14.1 us
  transfers between devices with their start and end apart: 3, of which 3 were waited for; matrix products, arithmetic and copies ran while one was open for 1% of the time, Pallas kernels for 0%

commit v1 on v0

--- a/solution.py
+++ b/solution.py
@@ -103,7 +103,8 @@
             lax.fori_loop(0, steps, add_block, jnp.zeros((2, heads, dir_count), jnp.float32))
         )
     partial_kochin = jnp.stack(kochin_parts)
-    kochin = lax.psum(partial_kochin, "panel")
+    pieces = lax.all_gather(partial_kochin, "panel")
+    kochin = jnp.sum(pieces, axis=0)
     cot = jnp.stack(
         [
             cotangent(kochin[freq], waves[freq], dir_ids, drift_cot[freq], heading_dir)

time: 539 us -> 520 us (0.965)
  waiting for transfers between devices: 224 us -> 201 us
    psum x1 -> x0, waiting for transfers between devices: 158 us -> none  [body(): kochin = lax.psum(partial_kochin, 'panel')]
    all_gather x0 -> x1, waiting for transfers between devices: none -> 135 us  [body(): pieces = lax.all_gather(partial_kochin, 'panel')]
where the time goes in v1:
time: 520 us; the launch traced here: 518 us
  other arithmetic  222 us (43%)
  waiting for transfers between devices  201 us (39%)
  local copies, waits for them, and re-layouts  52.7 us (10%)
  matrix products  19.1 us (4%)
  between operations  15.1 us (3%)
    all_gather x1, waiting for transfers between devices, body(): pieces = lax.all_gather(partial_kochin, 'panel')  135 us
    reduce_sum x16, other arithmetic, backward_block(): jnp.sum(twist * jnp.cos(angles)[None, :], 1)  85.8 us
    another operation x16, other arithmetic  74.9 us
    reduce_scatter x1, waiting for transfers between devices, body(): lax.psum_scatter(grads_all, 'dir', scatter_dimension=3, tiled=True)  35.9 us
    unnamed x4, waiting for transfers between devices  30.1 us
    slice x32, other arithmetic, phase_terms(): geometry[0][:, None] * jnp.cos(angles)[None, :]  27.5 us
    slice x16, local copies, waits for them, and re-layouts, add_block(): sig = lax.dynamic_slice_in_dim(sources[freq], start, block, 2)  20.7 us
    dynamic_update_slice x32, local copies, waits for them, and re-layouts, back_block(): grads_acc = lax.dynamic_update_slice_in_dim(grads_acc, dsig, start, 1)  14.1 us
  transfers between devices with their start and end apart: 3, of which 3 were waited for; matrix products, arithmetic and copies ran while one was open for 1% of the time, Pallas kernels for 0%

profile of v1, /device:TPU:8, one launch (start us, length us, event | category | flops | bytes accessed | tf_op | source)
XLA Modules:
  0.0 517.5 jit_solution(13872941885054928563)
XLA Ops:
  7.9 58.0 %while.74 = (s32[]{:T(128)}, f32[2,64,512]{2,1,0:T(8,128)S(1)}, bf16[2,2,64,4096]{3,2,1,0:T(8,128)(2,1)}, f32[4,4096]{1,0:T(4,128)}, f32[2]{0:T(128)S(1)}, /*ind...) while((s32[]{:T(128)}, f32[2,64,512]{2,1,0:T(8,128)S(1)}, ...), condition=%wide.region_1.0_spmd.clone, body=%wide.region_0.0_spmd.clone.sunk | while | flops 138677248 | bytes 6719737 | solution.py:103
  9.0 4.4 multiply_convert_fusion.6
  16.2 4.4 multiply_convert_fusion.6
  23.5 4.4 multiply_convert_fusion.6
  30.7 4.4 multiply_convert_fusion.6
  38.0 4.4 multiply_convert_fusion.6
  45.2 4.4 multiply_convert_fusion.6
  52.5 4.4 multiply_convert_fusion.6
  59.7 4.4 multiply_convert_fusion.6
  65.9 72.4 %while.75 = (s32[]{:T(128)}, f32[2,64,512]{2,1,0:T(8,128)S(1)}, bf16[2,2,64,4096]{3,2,1,0:T(8,128)(2,1)}, f32[4,4096]{1,0:T(4,128)}, f32[2]{0:T(128)S(1)}, /*ind...) while((s32[]{:T(128)}, f32[2,64,512]{2,1,0:T(8,128)S(1)}, ...), condition=%wide.region_3.0_spmd.clone, body=%wide.region_2.0_spmd.clone.sunk | while | flops 138677248 | bytes 6719745 | solution.py:103
  66.5 1.6 constant_dynamic-slice_fusion.23
  68.2 5.0 multiply_convert_fusion.7
  77.2 5.0 multiply_convert_fusion.7
  86.3 5.0 multiply_convert_fusion.7
  93.7 1.6 constant_dynamic-slice_fusion.23
  95.3 5.0 multiply_convert_fusion.7
  102.7 1.6 constant_dynamic-slice_fusion.23
  104.4 5.0 multiply_convert_fusion.7
  113.4 5.0 multiply_convert_fusion.7
  120.8 1.6 constant_dynamic-slice_fusion.23
  122.5 5.0 multiply_convert_fusion.7
  131.5 5.0 multiply_convert_fusion.7
  141.3 135.2 %all-gather.3.cloned.1.call-done = f32[32,2,64,512]{3,2,1,0:T(8,128)} async-done(((f32[2,2,64,512]{3,2,1,0:T(8,128)}), f32[32,2,64,512]{3,2,1,0:T(8,128)}) %all-gather.3.cloned.1.call-update) | async-done | bytes 8388624 | tf_op jit(solution)/shard_map/all_gather | solution.py:106
  276.5 4.4 reduce_sum.117
  281.2 1.6 broadcast.578.clone2
  282.8 59.4 %while.72 = (s32[]{:T(128)}, f32[128,4096]{1,0:T(8,128)}, f32[4,4096]{1,0:T(4,128)S(1)}, f32[4,4096]{1,0:T(4,128)S(1)}, f32[2]{0:T(128)S(1)}, /*index=5*/bf16[12...) while((s32[]{:T(128)}, f32[128,4096]{1,0:T(8,128)}, ...), condition=%wide.region_9.10_spmd.clone, body=%wide.region_5.9_spmd.clone.sunk | while | flops 275526656 | bytes 10699039 | solution.py:129
  283.6 5.1 multiply_reduce_fusion.6
  291.1 5.1 multiply_reduce_fusion.6
  298.5 5.1 multiply_reduce_fusion.6
  305.9 5.1 multiply_reduce_fusion.6
  313.3 5.1 multiply_reduce_fusion.6
  320.7 5.1 multiply_reduce_fusion.6
  328.2 5.1 multiply_reduce_fusion.6
  335.6 5.1 multiply_reduce_fusion.6
  343.8 88.5 %while.73 = (s32[]{:T(128)}, f32[128,4096]{1,0:T(8,128)}, f32[4,4096]{1,0:T(4,128)S(1)}, f32[4,4096]{1,0:T(4,128)S(1)}, f32[2]{0:T(128)S(1)}, /*index=5*/bf16[12...) while((s32[]{:T(128)}, f32[128,4096]{1,0:T(8,128)}, ...), condition=%wide.region_14.15_spmd.clone, body=%wide.region_10.14_spmd.clone.sunk | while | flops 275526656 | bytes 10699047 | solution.py:129
  345.8 5.7 %multiply_reduce_fusion.7 = (f32[512]{0:T(512)S(1)}, f32[512]{0:T(512)S(1)}, f32[512]{0:T(512)S(1)}, bf16[512,512]{1,0:T(8,128)(2,1)S(1)}, bf16[512,512]{1,0:T(8,128)(2,1)S(1)}) fusion(f32[512]{0:T(512)S(1)} %bitcast.252, f32[512]{0:T(512)S(1)} %bitcast.244, f32[512]{0:T(512)S(1)} %neg.91, f32[512,1024]{1,0:T(8,128)S(1)} %fusion.121, ...), kind=kLoop, calls=%fused_computation.39.clone.1 | loop fusion | flops 4979200 | bytes 3164164 | tf_op jit(solution)/shard_map/while/body/eval_jaxpr/reduce_sum | solution.py:75
  356.9 5.7 %multiply_reduce_fusion.7 = (f32[512]{0:T(512)S(1)}, f32[512]{0:T(512)S(1)}, f32[512]{0:T(512)S(1)}, bf16[512,512]{1,0:T(8,128)(2,1)S(1)}, bf16[512,512]{1,0:T(8,128)(2,1)S(1)}) fusion(f32[512]{0:T(512)S(1)} %bitcast.252, f32[512]{0:T(512)S(1)} %bitcast.244, f32[512]{0:T(512)S(1)} %neg.91, f32[512,1024]{1,0:T(8,128)S(1)} %fusion.121, ...), kind=kLoop, calls=%fused_computation.39.clone.1 | loop fusion | flops 4979200 | bytes 3164164 | tf_op jit(solution)/shard_map/while/body/eval_jaxpr/reduce_sum | solution.py:75
  367.9 5.7 %multiply_reduce_fusion.7 = (f32[512]{0:T(512)S(1)}, f32[512]{0:T(512)S(1)}, f32[512]{0:T(512)S(1)}, bf16[512,512]{1,0:T(8,128)(2,1)S(1)}, bf16[512,512]{1,0:T(8,128)(2,1)S(1)}) fusion(f32[512]{0:T(512)S(1)} %bitcast.252, f32[512]{0:T(512)S(1)} %bitcast.244, f32[512]{0:T(512)S(1)} %neg.91, f32[512,1024]{1,0:T(8,128)S(1)} %fusion.121, ...), kind=kLoop, calls=%fused_computation.39.clone.1 | loop fusion | flops 4979200 | bytes 3164164 | tf_op jit(solution)/shard_map/while/body/eval_jaxpr/reduce_sum | solution.py:75
  379.0 5.7 %multiply_reduce_fusion.7 = (f32[512]{0:T(512)S(1)}, f32[512]{0:T(512)S(1)}, f32[512]{0:T(512)S(1)}, bf16[512,512]{1,0:T(8,128)(2,1)S(1)}, bf16[512,512]{1,0:T(8,128)(2,1)S(1)}) fusion(f32[512]{0:T(512)S(1)} %bitcast.252, f32[512]{0:T(512)S(1)} %bitcast.244, f32[512]{0:T(512)S(1)} %neg.91, f32[512,1024]{1,0:T(8,128)S(1)} %fusion.121, ...), kind=kLoop, calls=%fused_computation.39.clone.1 | loop fusion | flops 4979200 | bytes 3164164 | tf_op jit(solution)/shard_map/while/body/eval_jaxpr/reduce_sum | solution.py:75
  390.1 5.7 %multiply_reduce_fusion.7 = (f32[512]{0:T(512)S(1)}, f32[512]{0:T(512)S(1)}, f32[512]{0:T(512)S(1)}, bf16[512,512]{1,0:T(8,128)(2,1)S(1)}, bf16[512,512]{1,0:T(8,128)(2,1)S(1)}) fusion(f32[512]{0:T(512)S(1)} %bitcast.252, f32[512]{0:T(512)S(1)} %bitcast.244, f32[512]{0:T(512)S(1)} %neg.91, f32[512,1024]{1,0:T(8,128)S(1)} %fusion.121, ...), kind=kLoop, calls=%fused_computation.39.clone.1 | loop fusion | flops 4979200 | bytes 3164164 | tf_op jit(solution)/shard_map/while/body/eval_jaxpr/reduce_sum | solution.py:75
  401.1 5.7 %multiply_reduce_fusion.7 = (f32[512]{0:T(512)S(1)}, f32[512]{0:T(512)S(1)}, f32[512]{0:T(512)S(1)}, bf16[512,512]{1,0:T(8,128)(2,1)S(1)}, bf16[512,512]{1,0:T(8,128)(2,1)S(1)}) fusion(f32[512]{0:T(512)S(1)} %bitcast.252, f32[512]{0:T(512)S(1)} %bitcast.244, f32[512]{0:T(512)S(1)} %neg.91, f32[512,1024]{1,0:T(8,128)S(1)} %fusion.121, ...), kind=kLoop, calls=%fused_computation.39.clone.1 | loop fusion | flops 4979200 | bytes 3164164 | tf_op jit(solution)/shard_map/while/body/eval_jaxpr/reduce_sum | solution.py:75
  412.2 5.7 %multiply_reduce_fusion.7 = (f32[512]{0:T(512)S(1)}, f32[512]{0:T(512)S(1)}, f32[512]{0:T(512)S(1)}, bf16[512,512]{1,0:T(8,128)(2,1)S(1)}, bf16[512,512]{1,0:T(8,128)(2,1)S(1)}) fusion(f32[512]{0:T(512)S(1)} %bitcast.252, f32[512]{0:T(512)S(1)} %bitcast.244, f32[512]{0:T(512)S(1)} %neg.91, f32[512,1024]{1,0:T(8,128)S(1)} %fusion.121, ...), kind=kLoop, calls=%fused_computation.39.clone.1 | loop fusion | flops 4979200 | bytes 3164164 | tf_op jit(solution)/shard_map/while/body/eval_jaxpr/reduce_sum | solution.py:75
  423.2 5.7 %multiply_reduce_fusion.7 = (f32[512]{0:T(512)S(1)}, f32[512]{0:T(512)S(1)}, f32[512]{0:T(512)S(1)}, bf16[512,512]{1,0:T(8,128)(2,1)S(1)}, bf16[512,512]{1,0:T(8,128)(2,1)S(1)}) fusion(f32[512]{0:T(512)S(1)} %bitcast.252, f32[512]{0:T(512)S(1)} %bitcast.244, f32[512]{0:T(512)S(1)} %neg.91, f32[512,1024]{1,0:T(8,128)S(1)} %fusion.121, ...), kind=kLoop, calls=%fused_computation.39.clone.1 | loop fusion | flops 4979200 | bytes 3164164 | tf_op jit(solution)/shard_map/while/body/eval_jaxpr/reduce_sum | solution.py:75
  432.3 2.0 copy.11
  434.4 4.0 pad_maximum_fusion
  438.4 30.1 %reduce-scatter.7.cloned.1.call-done = f32[512,4]{1,0:T(8,128)} async-done(((f32[4096,4]{1,0:T(8,128)}), f32[512,4]{1,0:T(8,128)}) %reduce-scatter.7.cloned.1.call-update) | async-done | bytes 8208
  469.5 5.0 psum.7
  475.1 35.9 %reduce-scatter.5.cloned.1.call-done = f32[2,2,64,512]{3,2,1,0:T(8,128)} async-done(((f32[2,2,64,4096]{3,2,1,0:T(8,128)}), f32[2,2,64,512]{3,2,1,0:T(8,128)}) %reduce-scatter.5.cloned.1.call-update) | async-done | bytes 524304 | tf_op jit(solution)/shard_map/reduce_scatter | solution.py:135
  (381 shorter events, 114.8 us)
Async XLA Ops:
  7.2 269.3 %all-gather.3.cloned.1.call-start = ((), (), s32[]{:S(2)}) async-start(), calls=%async_computation.3 | async-start | bytes 8912896 | tf_op jit(solution)/shard_map/all_gather | solution.py:106
  65.9 75.3 %copy-start.4 = (s32[64]{0:T(128)S(1)}, s32[64]{0:T(128)}, u32[]{:S(2)}) copy-start(s32[64]{0:T(128)} %param.17) | copy-start | bytes 772
  65.9 75.4 %copy-start.3 = (f32[2,64]{1,0:T(2,128)S(1)}, f32[2,64]{1,0:T(2,128)}, u32[]{:S(2)}) copy-start(f32[2,64]{1,0:T(2,128)} %param.15) | copy-start | bytes 1540
  139.2 329.3 %reduce-scatter.7.cloned.1.call-start = ((), (), s32[]{:S(2)}) async-start(), calls=%async_computation.4 | async-start | bytes 2359296
  280.9 1.9 copy-start
  280.9 1.9 copy-start.2
  432.3 2.1 copy-start.1
  434.3 76.7 %reduce-scatter.5.cloned.1.call-start = ((), (), s32[]{:S(2)}) async-start(), calls=%async_computation.2 | async-start | bytes 4718592 | tf_op jit(solution)/shard_map/reduce_scatter | solution.py:135
Sparse Core Ops, SparseCore 0:
  139.3 137.1 all-gather.2
  434.4 34.0 reduce-scatter.6
  471.6 39.3 reduce-scatter.4
